TPU v7x, 256 devices: a whole 4x4x8 slice. The times are simulated.
256 devices in a mesh: mic: 4 (over y), seq: 64 (over z, x, core).
Axes of the slice: x: 4, y: 4, z: 8, core: 2. Of those that a mesh axis runs over, the one named last changes fastest.
Arguments:
- frames_in: bfloat16 [8, 32768, 512], P('mic', 'seq'), may hold values from -16 to 16
- w_qkv: bfloat16 [8, 512, 1536], P('mic'), may hold values from -0.25 to 0.25
- w_join: bfloat16 [4096, 1024], P(('mic', 'seq')), may hold values from -0.09375 to 0.09375
- norm_gain: float32 [1024], replicated, may hold values from 0.5 to 2
- w_router: bfloat16 [1024, 64], replicated, may hold values from -0.1875 to 0.1875
- w_gate: bfloat16 [64, 1024, 4096], P('seq', None, 'mic'), may hold values from -0.1875 to 0.1875
- w_up: bfloat16 [64, 1024, 4096], P('seq', None, 'mic'), may hold values from -0.1875 to 0.1875
- w_down: bfloat16 [64, 4096, 1024], P('seq', 'mic'), may hold values from -0.09375 to 0.09375
- expert_ids: int32 [64, 4, 128, 2], P('seq', 'mic'), may hold values from 0 to 63, all different within a row; in each aligned block of 128 rows (0 to 127, 128 to 255, ..., all dimensions but the last counted through in order) at most 6 rows name the same one
Outputs:
- layer_out: bfloat16 [64, 4, 128, 1024], P('seq', 'mic')
Inputs may be any that keep to these rules, and one draw needn't show every extreme that they name: `expert_ids`: in the rows of one block (128 frames) no expert is named more than 6 times, a bound that some block reaches; the two ids of a frame differ.
All inputs are finite; a program needn't handle non-finite values.
Results may differ from a plain program's by a relative error of at most 0.017.
Values may be sent and summed in bfloat16 or wider, within the bound.
A program may use at most 128 MiB of HBM per device.

v0:
```python
import jax
import jax.numpy as jnp
from jax import lax
from jax.sharding import PartitionSpec as P

MICS = 8
HEADS = 8
TOP = 2


def body(frames_in, w_qkv, w_join, norm_gain, w_router, w_gate, w_up, w_down, expert_ids):
    mic_count = lax.axis_size("mic")
    seq_count = lax.axis_size("seq")
    mic_local, span, chan_width = frames_in.shape
    frame_rows = span // mic_count
    head_dim = chan_width // HEADS
    model_width = w_join.shape[1]
    expert_count = w_router.shape[1]
    exp_local = w_gate.shape[0]
    capacity = max(2, 3 * TOP * frame_rows // (2 * expert_count))
    projected = jnp.einsum(
        "mfc,mce->mfe", frames_in, w_qkv, preferred_element_type=jnp.float32
    ).astype(jnp.bfloat16)
    projected = projected.reshape(mic_local, mic_count, frame_rows, 3 * chan_width)
    arrived_block = lax.all_to_all(projected, "mic", split_axis=1, concat_axis=0, tiled=True)
    arrived_block = arrived_block[:, 0]
    frame_count = arrived_block.shape[1]
    queries = arrived_block[..., :chan_width].reshape(MICS, frame_count, HEADS, head_dim)
    keys_all = arrived_block[..., chan_width : 2 * chan_width].reshape(
        MICS, frame_count, HEADS, head_dim
    )
    values_all = arrived_block[..., 2 * chan_width :].reshape(MICS, frame_count, HEADS, head_dim)
    scores = jnp.einsum(
        "ifhd,jfhd->fhij", queries, keys_all, preferred_element_type=jnp.float32
    ) * head_dim ** (-0.5)
    row_max = jnp.max(scores, axis=-1, keepdims=True)
    weights = jnp.exp(scores - row_max)
    probs = (weights / jnp.sum(weights, axis=-1, keepdims=True)).astype(jnp.bfloat16)
    mixed_heads = jnp.einsum(
        "fhij,jfhd->fihd", probs, values_all, preferred_element_type=jnp.float32
    )
    attended = mixed_heads.astype(jnp.bfloat16).reshape(frame_count, MICS * chan_width)
    joined = jnp.dot(
        attended,
        lax.all_gather(w_join, ("mic", "seq"), axis=0, tiled=True),
        preferred_element_type=jnp.float32,
    )
    scale_row = lax.rsqrt(jnp.mean(joined * joined, axis=-1, keepdims=True) + 1e-06)
    normed = (joined * scale_row * norm_gain).astype(jnp.bfloat16)
    logits = jnp.dot(normed, w_router, preferred_element_type=jnp.float32)
    expert_rows = expert_ids.reshape(frame_rows, TOP)
    chosen = (expert_rows[..., None] == jnp.arange(expert_count, dtype=jnp.int32)).astype(jnp.int32)
    picked = jnp.sum(logits[:, None, :] * chosen.astype(jnp.float32), axis=-1)
    first_gate = 1.0 / (1.0 + jnp.exp(picked[:, 1] - picked[:, 0]))
    gates = jnp.stack([first_gate, 1.0 - first_gate], axis=-1)
    counts = jnp.sum(chosen, axis=1)
    before = jnp.cumsum(counts, axis=0) - counts
    slot_index = jnp.sum(before[:, None, :] * chosen, axis=-1)
    in_slot = slot_index[..., None] == jnp.arange(capacity, dtype=jnp.int32)
    mapped = (
        ((chosen[..., :, None] == 1) & in_slot[..., None, :])
        .reshape(frame_rows, TOP, expert_count * capacity)
        .astype(jnp.bfloat16)
    )
    merged_map = jnp.sum(mapped, axis=1)
    buffers = jnp.einsum(
        "rs,rd->sd", merged_map, normed, preferred_element_type=jnp.float32
    ).astype(jnp.bfloat16)
    buffers = buffers.reshape(seq_count, exp_local * capacity, model_width)
    landed = lax.all_to_all(buffers, "seq", split_axis=0, concat_axis=0, tiled=True)
    arrived = lax.all_gather(landed[None], "mic", axis=0, tiled=True)
    flat = arrived.reshape(mic_count * seq_count * exp_local * capacity, model_width)
    piece_rows = flat.reshape(-1, exp_local, capacity, model_width)
    first_proj = jnp.einsum(
        "nejd,edf->nejf", piece_rows, w_gate, preferred_element_type=jnp.float32
    )
    second_proj = jnp.einsum("nejd,edf->nejf", piece_rows, w_up, preferred_element_type=jnp.float32)
    inner = (jax.nn.silu(first_proj) * second_proj).astype(jnp.bfloat16)
    result = jnp.einsum("nejf,efd->nejd", inner, w_down, preferred_element_type=jnp.float32)
    summed = lax.psum_scatter(
        result.reshape(
            lax.axis_size("mic") * (seq_count * exp_local * capacity), model_width
        ).astype(jnp.bfloat16),
        "mic",
        scatter_dimension=0,
        tiled=True,
    ).astype(jnp.float32)
    summed = summed.astype(jnp.bfloat16).reshape(seq_count, exp_local * capacity, model_width)
    returned = lax.all_to_all(summed, "seq", split_axis=0, concat_axis=0, tiled=True)
    returned = returned.reshape(expert_count * capacity, model_width)
    picked_out = jnp.einsum("rks,sd->rkd", mapped, returned, preferred_element_type=jnp.float32)
    total = joined + jnp.sum(gates[..., None] * picked_out, axis=1)
    return total.astype(jnp.bfloat16).reshape(1, 1, frame_rows, model_width)


def solution(mesh):
    return jax.shard_map(
        body,
        mesh=mesh,
        in_specs=(
            P("mic", "seq", None),
            P("mic", None, None),
            P(("mic", "seq"), None),
            P(),
            P(),
            P("seq", None, "mic"),
            P("seq", None, "mic"),
            P("seq", "mic", None),
            P("seq", "mic", None, None),
        ),
        out_specs=P("seq", "mic", None, None),
        check_vma=False,
    )
```

profile of v0, /device:TPU:1, one launch (start us, length us, event | category | flops | bytes accessed | tf_op | source)
XLA Modules:
  0.0 346.4 jit_solution(7928431488291336185)
XLA Ops:
  6.5 0.0 copy-start
  6.5 0.0 all-gather.4.cloned.1.call-start
  6.5 0.7 all-gather.4.cloned.1.call-update
  7.3 1.2 copy-done
  8.4 3.0 convolution_convert_fusion
  11.5 2.0 copy.26
  13.4 0.0 copy-start.8
  13.4 5.1 %all-to-all-start = ((bf16[2,4,128,1536]{3,2,0,1:T(8,128)(2,1)}), bf16[2,4,128,1536]{3,2,0,1:T(8,128)(2,1)S(1)}, u32[]{:S(2)}, u32[]{:S(2)}) async-start(bf16[2,4,128,1536]{3,2,0,1:T(8,128)(2,1)} %copy.26), calls=%async_computation | async-start | bytes 6291456 | tf_op jit(solution)/shard_map/all_to_all | solution.py:25
  18.6 0.0 all-gather.6.cloned.1.call-start
  18.6 0.0 copy-done.8
  18.6 0.1 copy.35
  18.7 0.2 reduce_window_sum.11
  18.9 0.1 copy.37
  19.1 0.1 copy.38
  19.2 35.4 %all-to-all-done = bf16[2,4,128,1536]{3,2,0,1:T(8,128)(2,1)S(1)} async-done(((bf16[2,4,128,1536]{3,2,0,1:T(8,128)(2,1)}), bf16[2,4,128,1536]{3,2,0,1:T(8,128)(2,1)S(1)}, u32[]{:S(2)}, u32[]{:S(2)}) %all-to-all-start) | async-done | bytes 3145760 | tf_op jit(solution)/shard_map/all_to_all | solution.py:25
  54.6 1.7 fusion.37
  56.4 0.0 copy-start.4
  56.4 1.7 copy.28
  58.1 3.8 %copy.30 = bf16[8,128,8,64]{3,0,2,1:T(8,128)(2,1)} copy(bf16[8,128,8,64]{1,3,2,0:T(8,128)(2,1)S(1)} %bitcast.103) | data formatting | bytes 2097152 | tf_op jit(solution)/shard_map/reshape | solution.py:28
  61.8 0.0 copy-start.3
  61.8 0.0 copy-done.4
  61.8 0.7 copy.29
  62.5 3.7 %copy.31 = bf16[8,128,8,64]{3,0,2,1:T(8,128)(2,1)} copy(bf16[8,128,8,64]{1,3,2,0:T(8,128)(2,1)S(1)} %bitcast.104) | data formatting | bytes 2097152 | tf_op jit(solution)/shard_map/reshape | solution.py:29
  66.2 0.0 copy-done.3
  66.2 0.7 copy.27
  66.9 0.0 copy-start.5
  66.9 3.7 %copy.32 = bf16[8,128,8,64]{3,0,2,1:T(8,128)(2,1)} copy(bf16[8,128,8,64]{1,3,2,0:T(8,128)(2,1)S(1)} %bitcast.105) | data formatting | bytes 2097152 | tf_op jit(solution)/shard_map/reshape | solution.py:32
  70.6 0.0 copy-done.5
  70.6 6.6 %fusion.38 = (f32[128,8,8]{2,1,0:T(8,128)S(1)}, f32[128,8,8,8]{2,3,1,0:T(8,128)}) fusion(bf16[8,128,8,64]{3,0,2,1:T(8,128)(2,1)S(1)} %copy-done.5, bf16[8,128,8,64]{3,0,2,1:T(8,128)(2,1)} %copy.31), kind=kOutput, calls=%fused_computation.56 | convolution fusion | flops 8585223 | bytes 2392064 | tf_op jit(solution)/shard_map/sub | solution.py:37
  77.2 4.7 %convert_bitcast_fusion.1 = bf16[128,8,8,64]{3,1,2,0:T(8,128)(2,1)} fusion(bf16[8,128,8,64]{3,0,2,1:T(8,128)(2,1)} %copy.32, f32[128,8,8,8]{2,3,1,0:T(8,128)} %get-tuple-element.11, f32[128,8,8]{2,1,0:T(8,128)S(1)} %get-tuple-element.10), kind=kOutput, calls=%fused_computation.22 | convolution fusion | flops 9043968 | bytes 2392064 | tf_op jit(solution)/shard_map/fhij,jfhd->fihd/dot_general | solution.py:39
  81.9 3.2 copy.34
  85.1 59.5 %all-gather.4.cloned.1.call-done = bf16[4096,1024]{1,0:T(8,128)(2,1)} async-done(((bf16[16,1024]{1,0:T(8,128)(2,1)}), bf16[4096,1024]{1,0:T(8,128)(2,1)}) %all-gather.4.cloned.1.call-update) | async-done | bytes 8388624 | tf_op jit(solution)/shard_map/all_gather | solution.py:45
  144.6 0.0 copy-start.7
  144.6 4.7 %multiply_reduce_fusion.1 = (f32[128]{0:T(128)S(1)}, f32[128,1024]{1,0:T(8,128)S(1)}) fusion(bf16[128,4096]{0,1:T(8,128)(2,1)S(1)} %bitcast.102, bf16[4096,1024]{1,0:T(8,128)(2,1)} %all-gather.4.cloned.1.call-done), kind=kOutput, calls=%fused_computation.33 | convolution fusion | flops 1074003840 | bytes 9961984 | tf_op jit(solution)/shard_map/dot_general | solution.py:43
  149.3 0.0 copy-start.2
  149.3 0.0 copy-done.7
  149.3 0.4 convolution_convert_fusion.1
  149.8 0.3 reshape.92
  150.0 35.1 %all_to_all.25 = bf16[64,6,1024]{2,1,0:T(8,128)(2,1)S(1)} all-to-all(bf16[64,6,1024]{2,1,0:T(8,128)(2,1)S(1)} %reshape.92), channel_id=1, replica_groups=mesh['mic'=4,'seq'=64] {'seq'}, dimensions={0} | all-to-all | bytes 1572864 | tf_op jit(solution)/shard_map/all_to_all | solution.py:70
  185.1 1.3 copy.39
  186.4 0.0 copy-done.2
  186.4 0.0 all-gather.6.cloned.1.call-update
  186.5 0.0 reduce-scatter.2.cloned.1.call-start
  186.5 37.7 %all-gather.6.cloned.1.call-done = bf16[256,6,1024]{2,0,1:T(8,128)(2,1)} async-done(((bf16[64,6,1024]{2,0,1:T(8,128)(2,1)}), bf16[256,6,1024]{2,0,1:T(8,128)(2,1)}) %all-gather.6.cloned.1.call-update) | async-done | bytes 3145744 | tf_op jit(solution)/shard_map/all_gather | solution.py:71
  224.2 8.6 %fusion.19 = f32[256,6,1024]{2,0,1:T(8,128)} fusion(bf16[256,6,1024]{2,0,1:T(8,128)(2,1)} %all-gather.6.cloned.1.call-done, bf16[1,1024,1024]{2,1,0:T(8,128)(2,1)} %param.14), kind=kOutput, calls=%fused_computation.20 | convolution fusion | flops 3221225472 | bytes 11534336 | tf_op jit(solution)/shard_map/nejd,edf->nejf/dot_general | solution.py:74
  232.8 10.6 %convert_bitcast_fusion = bf16[256,1,6,1024]{3,0,2,1:T(8,128)(2,1)S(1)} fusion(f32[256,6,1024]{2,0,1:T(8,128)} %fusion.19, bf16[256,6,1024]{2,0,1:T(8,128)(2,1)} %all-gather.6.cloned.1.call-done, bf16[1,1024,1024]{2,1,0:T(8,128)(2,1)} %param.16, bf16[1,1024,1024]{2,1,0:T(8,128)(2,1)} %param.15), kind=kOutput, calls=%fused_computation.15 | convolution fusion | flops 6453460992 | bytes 16777216 | tf_op jit(solution)/shard_map/nejf,efd->nejd/dot_general | solution.py:79
  243.4 3.7 %copy.40 = bf16[256,1,6,1024]{3,2,0,1:T(8,128)(2,1)} copy(bf16[256,1,6,1024]{3,0,2,1:T(8,128)(2,1)S(1)} %convert_bitcast_fusion) | data formatting | bytes 6291456 | tf_op jit(solution)/shard_map/convert_element_type | solution.py:83
  247.1 6.3 %convert_element_type.71 = bf16[1536,1024]{1,0:T(8,128)(2,1)} reshape(bf16[256,1,6,1024]{3,2,0,1:T(8,128)(2,1)} %copy.40) | data formatting | bytes 6291456 | tf_op jit(solution)/shard_map/convert_element_type | solution.py:83
  253.4 0.0 copy-start.6
  253.4 0.0 reduce-scatter.2.cloned.1.call-update
  253.5 41.3 %reduce-scatter.2.cloned.1.call-done = bf16[384,1024]{1,0:T(8,128)(2,1)} async-done(((bf16[1536,1024]{1,0:T(8,128)(2,1)}), bf16[384,1024]{1,0:T(8,128)(2,1)}) %reduce-scatter.2.cloned.1.call-update) | async-done | bytes 786448 | tf_op jit(solution)/shard_map/reduce_scatter | solution.py:80
  294.7 0.0 copy-start.1
  294.7 2.3 reshape.98
  297.1 10.8 %all-to-all-start.2 = ((bf16[64,6,1024]{2,1,0:T(8,128)(2,1)}), bf16[64,6,1024]{2,1,0:T(8,128)(2,1)}, u32[]{:S(2)}, u32[]{:S(2)}) async-start(bf16[64,6,1024]{2,1,0:T(8,128)(2,1)} %reshape.98), calls=%async_computation.3 | async-start | bytes 2097152 | tf_op jit(solution)/shard_map/all_to_all | solution.py:89
  307.9 0.0 copy-done.6
  307.9 1.3 fusion.36
  309.3 26.5 %all-to-all-done.2 = bf16[64,6,1024]{2,1,0:T(8,128)(2,1)} async-done(((bf16[64,6,1024]{2,1,0:T(8,128)(2,1)}), bf16[64,6,1024]{2,1,0:T(8,128)(2,1)}, u32[]{:S(2)}, u32[]{:S(2)}) %all-to-all-start.2) | async-done | bytes 786464 | tf_op jit(solution)/shard_map/all_to_all | solution.py:89
  335.8 2.3 fusion.24
  338.1 1.8 fusion.28
  339.9 0.0 copy-done.1
  (11 shorter events, 0.2 us)
Async XLA Ops:
  6.5 1.9 copy-start
  6.5 138.0 %all-gather.4.cloned.1.call-start = ((), (), s32[]{:S(2)}) async-start(), calls=%async_computation.4 | async-start | bytes 8421376 | tf_op jit(solution)/shard_map/all_gather | solution.py:45
  13.4 5.2 %copy-start.8 = (s32[1,1,128,2]{2,3,1,0:T(2,128)S(1)}, s32[1,1,128,2]{2,3,1,0:T(2,128)}, u32[]{:S(2)}) copy-start(s32[1,1,128,2]{2,3,1,0:T(2,128)} %param.17) | copy-start | bytes 3076
  13.4 41.2 %all-to-all-start = ((bf16[2,4,128,1536]{3,2,0,1:T(8,128)(2,1)}), bf16[2,4,128,1536]{3,2,0,1:T(8,128)(2,1)S(1)}, u32[]{:S(2)}, u32[]{:S(2)}) async-start(bf16[2,4,128,1536]{3,2,0,1:T(8,128)(2,1)} %copy.26), calls=%async_computation | async-start | bytes 6291456 | tf_op jit(solution)/shard_map/all_to_all | solution.py:25
  18.6 205.6 %all-gather.6.cloned.1.call-start = ((), (), s32[]{:S(2)}) async-start(), calls=%async_computation.6 | async-start | bytes 3932160 | tf_op jit(solution)/shard_map/all_gather | solution.py:71
  56.4 5.5 %copy-start.4 = (bf16[8,128,512]{2,1,0:T(8,128)(2,1)S(1)}, bf16[8,128,512]{2,1,0:T(8,128)(2,1)}, u32[]{:S(2)}) copy-start(bf16[8,128,512]{2,1,0:T(8,128)(2,1)} %get-tuple-element.7) | copy-start | bytes 3145732
  61.8 4.4 %copy-start.3 = (bf16[8,128,512]{2,1,0:T(8,128)(2,1)S(1)}, bf16[8,128,512]{2,1,0:T(8,128)(2,1)}, u32[]{:S(2)}) copy-start(bf16[8,128,512]{2,1,0:T(8,128)(2,1)} %get-tuple-element.9) | copy-start | bytes 3145732
  66.9 3.8 %copy-start.5 = (bf16[8,128,8,64]{3,0,2,1:T(8,128)(2,1)S(1)}, bf16[8,128,8,64]{3,0,2,1:T(8,128)(2,1)}, u32[]{:S(2)}) copy-start(bf16[8,128,8,64]{3,0,2,1:T(8,128)(2,1)} %copy.30) | copy-start | bytes 3145732
  144.6 4.8 %copy-start.7 = (f32[1024]{0:T(1024)S(1)}, f32[1024]{0:T(1024)}, u32[]{:S(2)}) copy-start(f32[1024]{0:T(1024)} %param.12) | copy-start | bytes 12292
  149.3 37.1 %copy-start.2 = (f32[128,1024]{1,0:T(8,128)}, f32[128,1024]{1,0:T(8,128)S(1)}, u32[]{:S(2)}) copy-start(f32[128,1024]{1,0:T(8,128)S(1)} %get-tuple-element.13) | copy-start | bytes 1572868
  186.5 108.3 %reduce-scatter.2.cloned.1.call-start = ((), (), s32[]{:S(2)}) async-start(), calls=%async_computation.5 | async-start | bytes 3932160 | tf_op jit(solution)/shard_map/reduce_scatter | solution.py:80
  253.4 54.4 %copy-start.6 = (bf16[1024,64]{0,1:T(8,128)(2,1)S(1)}, bf16[1024,64]{0,1:T(8,128)(2,1)}, u32[]{:S(2)}) copy-start(bf16[1024,64]{0,1:T(8,128)(2,1)} %param.13) | copy-start | bytes 393220
  294.7 45.2 %copy-start.1 = (bf16[2,512,1536]{2,1,0:T(8,128)(2,1)S(1)}, bf16[2,512,1536]{2,1,0:T(8,128)(2,1)}, u32[]{:S(2)}) copy-start(bf16[2,512,1536]{2,1,0:T(8,128)(2,1)} %param.10) | copy-start | bytes 9437188
  297.1 38.7 %all-to-all-start.2 = ((bf16[64,6,1024]{2,1,0:T(8,128)(2,1)}), bf16[64,6,1024]{2,1,0:T(8,128)(2,1)}, u32[]{:S(2)}, u32[]{:S(2)}) async-start(bf16[64,6,1024]{2,1,0:T(8,128)(2,1)} %reshape.98), calls=%async_computation.3 | async-start | bytes 2097152 | tf_op jit(solution)/shard_map/all_to_all | solution.py:89
Sparse Core Ops, SparseCore 0:
  10.9 133.5 all-gather.3
  186.6 37.5 all-gather.5
  253.6 41.0 reduce-scatter.1
where the time goes:
time: 347 us; the launch traced here: 346 us
  waiting for transfers between devices  201 us (58%)
  matrix products  42.3 us (12%)
  local copies, waits for them, and re-layouts  36.6 us (11%)
  blocking collectives  35.1 us (10%)
  starting transfers between devices  16 us (5%)
  between operations  13.3 us (4%)
    all_gather x1, waiting for transfers between devices, body(): lax.all_gather(w_join, ('mic', 'seq'), axis=0, tiled=True)  59.5 us
    reduce_scatter x1, waiting for transfers between devices, body(): lax.psum_scatter(result.reshape(lax.axis_size('mic') * (seq_count * exp_l...  41.3 us
    all_gather x1, waiting for transfers between devices, body(): arrived = lax.all_gather(landed[None], 'mic', axis=0, tiled=True)  37.7 us
    all_to_all x1, waiting for transfers between devices, body(): lax.all_to_all(projected, 'mic', split_axis=1, concat_axis=0, tiled=True)  35.4 us
    all_to_all x1, blocking collectives, body(): lax.all_to_all(buffers, 'seq', split_axis=0, concat_axis=0, tiled=True)  35.1 us
    all_to_all x1, waiting for transfers between devices, body(): lax.all_to_all(summed, 'seq', split_axis=0, concat_axis=0, tiled=True)  26.5 us
    all_to_all x1, starting transfers between devices, body(): lax.all_to_all(summed, 'seq', split_axis=0, concat_axis=0, tiled=True)  10.8 us
    dot_general x1, matrix products, body(): jnp.einsum('nejf,efd->nejd', inner, w_down, preferred_element_type=jnp.fl...  10.6 us
  transfers between devices with their start and end apart: 5, of which 5 were waited for; matrix products, arithmetic and copies ran while one was open for 11% of the time, Pallas kernels for 0%

commit v1 on v0

--- a/solution.py
+++ b/solution.py
@@ -6,6 +6,36 @@
 MICS = 8
 HEADS = 8
 TOP = 2
+
+
+def watch_forms(load, which_dim):
+    axis_key = "mic"
+    shaped = jax.lax.axis_size(axis_key)
+    ready = jax.lax.axis_index(axis_key)
+    z2, current_arr, heard = (shaped, ready, load.shape[which_dim])
+    line_up = [(jj, (jj + 1) % z2) for jj in range(z2)]
+    parts_seen = [(jj, (jj - 1) % z2) for jj in range(z2)]
+    block_out = jnp.zeros(
+        (*load.shape[:which_dim], z2 * heard, *load.shape[which_dim + 1 :]), load.dtype
+    )
+    block_out = lax.dynamic_update_slice_in_dim(
+        block_out, load, current_arr * heard, axis=which_dim
+    )
+    t_next = z_new = load
+    response = z2 // 2
+    w = 1
+    while w < response + 1:
+        t_next = jax.lax.ppermute(t_next, axis_name=axis_key, perm=line_up)
+        block_out = lax.dynamic_update_slice_in_dim(
+            block_out, t_next, (current_arr - w) % z2 * heard, axis=which_dim
+        )
+        if w < z2 - response:
+            z_new = jax.lax.ppermute(z_new, axis_name=axis_key, perm=parts_seen)
+            block_out = lax.dynamic_update_slice_in_dim(
+                block_out, z_new, (current_arr + w) % z2 * heard, axis=which_dim
+            )
+        w += 1
+    return block_out
 
 
 def body(frames_in, w_qkv, w_join, norm_gain, w_router, w_gate, w_up, w_down, expert_ids):
@@ -68,7 +98,7 @@
     ).astype(jnp.bfloat16)
     buffers = buffers.reshape(seq_count, exp_local * capacity, model_width)
     landed = lax.all_to_all(buffers, "seq", split_axis=0, concat_axis=0, tiled=True)
-    arrived = lax.all_gather(landed[None], "mic", axis=0, tiled=True)
+    arrived = watch_forms(landed[None], 0)
     flat = arrived.reshape(mic_count * seq_count * exp_local * capacity, model_width)
     piece_rows = flat.reshape(-1, exp_local, capacity, model_width)
     first_proj = jnp.einsum(

time: 347 us -> 342 us (0.986)
  waiting for transfers between devices: 201 us -> 193 us
    all_gather x1 -> x0, waiting for transfers between devices: 37.7 us -> none  [body(): arrived = lax.all_gather(landed[None], 'mic', axis=0, tiled=True)]
    ppermute x0 -> x3, waiting for transfers between devices: none -> 32 us  [the longest x2 31.9 us: watch_forms(): t_next = jax.lax.ppermute(t_next, axis_name=axis_key, perm=line_up)]
  transfers between devices with their start and end apart: 5 -> 7, of which waited for: 5 -> 6; matrix products, arithmetic and copies ran while one was open for 11% -> 12% of each run, Pallas kernels for 0% -> 0%
where the time goes in v1:
time: 342 us
  waiting for transfers between devices  193 us (56%)
  local copies, waits for them, and re-layouts  40 us (12%)
  matrix products  38.9 us (11%)
  blocking collectives  35.1 us (10%)
  starting transfers between devices  18.7 us (5%)
  between operations  13.6 us (4%)
    all_gather x1, waiting for transfers between devices, body(): lax.all_gather(w_join, ('mic', 'seq'), axis=0, tiled=True)  59.5 us
    reduce_scatter x1, waiting for transfers between devices, body(): lax.psum_scatter(result.reshape(lax.axis_size('mic') * (seq_count * exp_l...  39.1 us
    all_to_all x1, waiting for transfers between devices, body(): lax.all_to_all(projected, 'mic', split_axis=1, concat_axis=0, tiled=True)  35.4 us
    all_to_all x1, blocking collectives, body(): lax.all_to_all(buffers, 'seq', split_axis=0, concat_axis=0, tiled=True)  35.1 us
    ppermute x2, waiting for transfers between devices, watch_forms(): t_next = jax.lax.ppermute(t_next, axis_name=axis_key, perm=line_up)  31.9 us
    all_to_all x1, waiting for transfers between devices, body(): lax.all_to_all(summed, 'seq', split_axis=0, concat_axis=0, tiled=True)  26.5 us
    all_to_all x1, starting transfers between devices, body(): lax.all_to_all(summed, 'seq', split_axis=0, concat_axis=0, tiled=True)  10.8 us
    dot_general x1, matrix products, body(): jnp.einsum('nejf,efd->nejd', inner, w_down, preferred_element_type=jnp.fl...  10.6 us
  transfers between devices with their start and end apart: 7, of which 6 were waited for; matrix products, arithmetic and copies ran while one was open for 12% of the time, Pallas kernels for 0%

profile of v1, /device:TPU:1, one launch (start us, length us, event | category | flops | bytes accessed | tf_op | source)
XLA Modules:
  0.0 341.7 jit_solution(9862878899361845598)
XLA Ops:
  6.5 0.0 copy-start
  6.5 0.0 all-gather.2.cloned.1.call-start
  6.5 0.7 all-gather.2.cloned.1.call-update
  7.3 1.2 copy-done
  8.4 3.0 convolution_convert_fusion
  11.5 2.0 copy.32
  13.4 5.1 %all-to-all-start = ((bf16[2,4,128,1536]{3,2,0,1:T(8,128)(2,1)}), bf16[2,4,128,1536]{3,2,0,1:T(8,128)(2,1)S(1)}, u32[]{:S(2)}, u32[]{:S(2)}) async-start(bf16[2,4,128,1536]{3,2,0,1:T(8,128)(2,1)} %copy.32), calls=%async_computation | async-start | bytes 6291456 | tf_op jit(solution)/shard_map/all_to_all | solution.py:55
  18.6 0.0 reduce-scatter.2.cloned.1.call-start
  18.6 0.0 copy-done.9
  18.6 0.1 copy.41
  18.7 0.2 reduce_window_sum.11
  18.9 0.1 copy.43
  19.1 0.1 copy.44
  19.2 35.4 %all-to-all-done = bf16[2,4,128,1536]{3,2,0,1:T(8,128)(2,1)S(1)} async-done(((bf16[2,4,128,1536]{3,2,0,1:T(8,128)(2,1)}), bf16[2,4,128,1536]{3,2,0,1:T(8,128)(2,1)S(1)}, u32[]{:S(2)}, u32[]{:S(2)}) %all-to-all-start) | async-done | bytes 3145760 | tf_op jit(solution)/shard_map/all_to_all | solution.py:55
  54.6 1.7 fusion.37
  56.4 1.7 copy.34
  58.1 3.8 %copy.36 = bf16[8,128,8,64]{3,0,2,1:T(8,128)(2,1)} copy(bf16[8,128,8,64]{1,3,2,0:T(8,128)(2,1)S(1)} %bitcast.113) | data formatting | bytes 2097152 | tf_op jit(solution)/shard_map/reshape | solution.py:58
  61.8 0.0 copy-done.4
  61.8 0.7 copy.35
  62.5 3.7 %copy.37 = bf16[8,128,8,64]{3,0,2,1:T(8,128)(2,1)} copy(bf16[8,128,8,64]{1,3,2,0:T(8,128)(2,1)S(1)} %bitcast.114) | data formatting | bytes 2097152 | tf_op jit(solution)/shard_map/reshape | solution.py:59
  66.2 0.0 copy-done.3
  66.2 0.7 copy.33
  66.9 0.0 copy-start.6
  66.9 3.7 %copy.38 = bf16[8,128,8,64]{3,0,2,1:T(8,128)(2,1)} copy(bf16[8,128,8,64]{1,3,2,0:T(8,128)(2,1)S(1)} %bitcast.115) | data formatting | bytes 2097152 | tf_op jit(solution)/shard_map/reshape | solution.py:62
  70.6 0.0 copy-done.6
  70.6 6.6 %fusion.38 = (f32[128,8,8]{2,1,0:T(8,128)S(1)}, f32[128,8,8,8]{2,3,1,0:T(8,128)}) fusion(bf16[8,128,8,64]{3,0,2,1:T(8,128)(2,1)S(1)} %copy-done.6, bf16[8,128,8,64]{3,0,2,1:T(8,128)(2,1)} %copy.37), kind=kOutput, calls=%fused_computation.60 | convolution fusion | flops 8585223 | bytes 2392064 | tf_op jit(solution)/shard_map/sub | solution.py:67
  77.2 4.7 %convert_bitcast_fusion.1 = bf16[128,8,8,64]{3,1,2,0:T(8,128)(2,1)} fusion(bf16[8,128,8,64]{3,0,2,1:T(8,128)(2,1)} %copy.38, f32[128,8,8,8]{2,3,1,0:T(8,128)} %get-tuple-element.11, f32[128,8,8]{2,1,0:T(8,128)S(1)} %get-tuple-element.10), kind=kOutput, calls=%fused_computation.22 | convolution fusion | flops 9043968 | bytes 2392064 | tf_op jit(solution)/shard_map/fhij,jfhd->fihd/dot_general | solution.py:69
  81.9 3.2 copy.40
  85.1 59.5 %all-gather.2.cloned.1.call-done = bf16[4096,1024]{1,0:T(8,128)(2,1)} async-done(((bf16[16,1024]{1,0:T(8,128)(2,1)}), bf16[4096,1024]{1,0:T(8,128)(2,1)}) %all-gather.2.cloned.1.call-update) | async-done | bytes 8388624 | tf_op jit(solution)/shard_map/all_gather | solution.py:75
  144.6 4.7 %multiply_reduce_fusion.1 = (f32[128]{0:T(128)S(1)}, f32[128,1024]{1,0:T(8,128)S(1)}) fusion(bf16[128,4096]{0,1:T(8,128)(2,1)S(1)} %bitcast.112, bf16[4096,1024]{1,0:T(8,128)(2,1)} %all-gather.2.cloned.1.call-done), kind=kOutput, calls=%fused_computation.37 | convolution fusion | flops 1074003840 | bytes 9961984 | tf_op jit(solution)/shard_map/dot_general | solution.py:73
  149.3 0.0 copy-done.8
  149.3 0.4 convolution_convert_fusion.1
  149.8 0.3 copy-done.2
  150.1 0.3 reshape.92
  150.4 35.1 %all_to_all.25 = bf16[64,6,1024]{2,1,0:T(8,128)(2,1)S(1)} all-to-all(bf16[64,6,1024]{2,1,0:T(8,128)(2,1)S(1)} %reshape.92), channel_id=1, replica_groups=mesh['mic'=4,'seq'=64] {'seq'}, dimensions={0} | all-to-all | bytes 1572864 | tf_op jit(solution)/shard_map/all_to_all | solution.py:100
  185.5 0.4 copy.46
  185.9 0.1 collective-permute-start
  186.0 2.7 collective-permute-start.1
  188.6 16.2 %collective-permute-done = bf16[1,64,6,1024]{3,1,2,0:T(8,128)(2,1)S(1)} collective-permute-done((bf16[1,64,6,1024]{3,1,2,0:T(8,128)(2,1)S(1)}, bf16[1,64,6,1024]{3,1,2,0:T(8,128)(2,1)S(1)}, u32[]{:S(2)}, u32[]{:S(2)}) %collective-permute-start) | collective-permute-done | bytes 786464 | tf_op jit(solution)/shard_map/ppermute | solution.py:28
  204.9 0.0 collective-permute-start.2
  204.9 0.4 broadcast_in_dim.4
  205.2 0.0 copy-start.10
  205.3 0.5 copy_dynamic-update-slice_fusion
  205.8 0.1 bitcast_dynamic-update-slice_fusion.2
  205.8 0.0 collective-permute-done.1
  205.8 1.2 bitcast_dynamic-update-slice_fusion.1
  207.1 15.7 %collective-permute-done.2 = bf16[1,64,6,1024]{3,1,2,0:T(8,128)(2,1)S(1)} collective-permute-done((bf16[1,64,6,1024]{3,1,2,0:T(8,128)(2,1)S(1)}, bf16[1,64,6,1024]{3,1,2,0:T(8,128)(2,1)S(1)}, u32[]{:S(2)}, u32[]{:S(2)}) %collective-permute-start.2) | collective-permute-done | bytes 786464 | tf_op jit(solution)/shard_map/ppermute | solution.py:28
  222.8 0.1 bitcast_dynamic-update-slice_fusion
  222.9 0.0 copy-start.5
  222.9 1.7 copy-done.5
  224.6 0.0 copy-done.10
  224.6 5.3 %fusion.19 = f32[256,6,1024]{2,0,1:T(8,128)} fusion(bf16[256,6,1024]{2,0,1:T(8,128)(2,1)S(1)} %bitcast.117, bf16[1,1024,1024]{2,1,0:T(8,128)(2,1)S(1)} %copy-done.10), kind=kOutput, calls=%fused_computation.20 | convolution fusion | flops 3221225472 | bytes 11534336 | tf_op jit(solution)/shard_map/nejd,edf->nejf/dot_general | solution.py:104
  229.9 10.6 %convert_bitcast_fusion = bf16[256,1,6,1024]{3,0,2,1:T(8,128)(2,1)S(1)} fusion(f32[256,6,1024]{2,0,1:T(8,128)} %fusion.19, bf16[256,6,1024]{2,0,1:T(8,128)(2,1)} %bitcast.118, bf16[1,1024,1024]{2,1,0:T(8,128)(2,1)} %param.16, bf16[1,1024,1024]{2,1,0:T(8,128)(2,1)} %param.15), kind=kOutput, calls=%fused_computation.15 | convolution fusion | flops 6453460992 | bytes 16777216 | tf_op jit(solution)/shard_map/nejf,efd->nejd/dot_general | solution.py:109
  240.4 3.7 %copy.51 = bf16[256,1,6,1024]{3,2,0,1:T(8,128)(2,1)} copy(bf16[256,1,6,1024]{3,0,2,1:T(8,128)(2,1)S(1)} %convert_bitcast_fusion) | data formatting | bytes 6291456 | tf_op jit(solution)/shard_map/convert_element_type | solution.py:113
  244.2 6.3 %convert_element_type.71 = bf16[1536,1024]{1,0:T(8,128)(2,1)} reshape(bf16[256,1,6,1024]{3,2,0,1:T(8,128)(2,1)} %copy.51) | data formatting | bytes 6291456 | tf_op jit(solution)/shard_map/convert_element_type | solution.py:113
  250.5 0.0 reduce-scatter.2.cloned.1.call-update
  250.5 39.1 %reduce-scatter.2.cloned.1.call-done = bf16[384,1024]{1,0:T(8,128)(2,1)} async-done(((bf16[1536,1024]{1,0:T(8,128)(2,1)}), bf16[384,1024]{1,0:T(8,128)(2,1)}) %reduce-scatter.2.cloned.1.call-update) | async-done | bytes 786448 | tf_op jit(solution)/shard_map/reduce_scatter | solution.py:110
  289.7 2.3 reshape.98
  292.0 10.8 %all-to-all-start.2 = ((bf16[64,6,1024]{2,1,0:T(8,128)(2,1)}), bf16[64,6,1024]{2,1,0:T(8,128)(2,1)}, u32[]{:S(2)}, u32[]{:S(2)}) async-start(bf16[64,6,1024]{2,1,0:T(8,128)(2,1)} %reshape.98), calls=%async_computation.3 | async-start | bytes 2097152 | tf_op jit(solution)/shard_map/all_to_all | solution.py:119
  302.8 0.0 copy-done.7
  302.8 1.3 fusion.36
  304.2 26.5 %all-to-all-done.2 = bf16[64,6,1024]{2,1,0:T(8,128)(2,1)} async-done(((bf16[64,6,1024]{2,1,0:T(8,128)(2,1)}), bf16[64,6,1024]{2,1,0:T(8,128)(2,1)}, u32[]{:S(2)}, u32[]{:S(2)}) %all-to-all-start.2) | async-done | bytes 786464 | tf_op jit(solution)/shard_map/all_to_all | solution.py:119
  330.7 2.3 fusion.24
  333.0 1.8 fusion.28
  (19 shorter events, 0.2 us)
Async XLA Ops:
  6.5 1.9 copy-start
  6.5 138.0 %all-gather.2.cloned.1.call-start = ((), (), s32[]{:S(2)}) async-start(), calls=%async_computation.4 | async-start | bytes 8421376 | tf_op jit(solution)/shard_map/all_gather | solution.py:75
  13.4 5.2 %copy-start.9 = (s32[1,1,128,2]{2,3,1,0:T(2,128)S(1)}, s32[1,1,128,2]{2,3,1,0:T(2,128)}, u32[]{:S(2)}) copy-start(s32[1,1,128,2]{2,3,1,0:T(2,128)} %param.17) | copy-start | bytes 3076
  13.4 41.2 %all-to-all-start = ((bf16[2,4,128,1536]{3,2,0,1:T(8,128)(2,1)}), bf16[2,4,128,1536]{3,2,0,1:T(8,128)(2,1)S(1)}, u32[]{:S(2)}, u32[]{:S(2)}) async-start(bf16[2,4,128,1536]{3,2,0,1:T(8,128)(2,1)} %copy.32), calls=%async_computation | async-start | bytes 6291456 | tf_op jit(solution)/shard_map/all_to_all | solution.py:55
  18.6 271.1 %reduce-scatter.2.cloned.1.call-start = ((), (), s32[]{:S(2)}) async-start(), calls=%async_computation.5 | async-start | bytes 3932160 | tf_op jit(solution)/shard_map/reduce_scatter | solution.py:110
  56.4 5.5 %copy-start.4 = (bf16[8,128,512]{2,1,0:T(8,128)(2,1)S(1)}, bf16[8,128,512]{2,1,0:T(8,128)(2,1)}, u32[]{:S(2)}) copy-start(bf16[8,128,512]{2,1,0:T(8,128)(2,1)} %get-tuple-element.7) | copy-start | bytes 3145732
  61.8 4.4 %copy-start.3 = (bf16[8,128,512]{2,1,0:T(8,128)(2,1)S(1)}, bf16[8,128,512]{2,1,0:T(8,128)(2,1)}, u32[]{:S(2)}) copy-start(bf16[8,128,512]{2,1,0:T(8,128)(2,1)} %get-tuple-element.9) | copy-start | bytes 3145732
  66.9 3.8 %copy-start.6 = (bf16[8,128,8,64]{3,0,2,1:T(8,128)(2,1)S(1)}, bf16[8,128,8,64]{3,0,2,1:T(8,128)(2,1)}, u32[]{:S(2)}) copy-start(bf16[8,128,8,64]{3,0,2,1:T(8,128)(2,1)} %copy.36) | copy-start | bytes 3145732
  144.6 4.8 %copy-start.8 = (f32[1024]{0:T(1024)S(1)}, f32[1024]{0:T(1024)}, u32[]{:S(2)}) copy-start(f32[1024]{0:T(1024)} %param.12) | copy-start | bytes 12292
  149.3 0.8 copy-start.2
  185.9 19.0 %collective-permute-start = (bf16[1,64,6,1024]{3,1,2,0:T(8,128)(2,1)S(1)}, bf16[1,64,6,1024]{3,1,2,0:T(8,128)(2,1)S(1)}, u32[]{:S(2)}, u32[]{:S(2)}) collective-permute-start(bf16[1,64,6,1024]{3,1,2,0:T(8,128)(2,1)S(1)} %copy.46), channel_id=1, source_target_pairs={{0,64},{64,128},{128,192},{192,0},{1,65},{65,129},{129,193},{193,1... | collective-permute-start | bytes 2359304 | tf_op jit(solution)/shard_map/ppermute | solution.py:28
  186.0 19.8 %collective-permute-start.1 = (bf16[1,64,6,1024]{3,1,2,0:T(8,128)(2,1)S(1)}, bf16[1,64,6,1024]{3,1,2,0:T(8,128)(2,1)}, u32[]{:S(2)}, u32[]{:S(2)}) collective-permute-start(bf16[1,64,6,1024]{3,1,2,0:T(8,128)(2,1)S(1)} %copy.46), channel_id=1, source_target_pairs={{0,192},{64,0},{128,64},{192,128},{1,193},{65,1},{129,65},{193,129... | collective-permute-start | bytes 2359304 | tf_op jit(solution)/shard_map/ppermute | solution.py:33
  204.9 18.0 %collective-permute-start.2 = (bf16[1,64,6,1024]{3,1,2,0:T(8,128)(2,1)S(1)}, bf16[1,64,6,1024]{3,1,2,0:T(8,128)(2,1)S(1)}, u32[]{:S(2)}, u32[]{:S(2)}) collective-permute-start(bf16[1,64,6,1024]{3,1,2,0:T(8,128)(2,1)S(1)} %collective-permute-done), channel_id=1, source_target_pairs={{0,64},{64,128},{128,192},{192,0},{1,65},{65,129},{129,193},{193,1... | collective-permute-start | bytes 2359304 | tf_op jit(solution)/shard_map/ppermute | solution.py:28
  205.2 19.3 %copy-start.10 = (bf16[1,1024,1024]{2,1,0:T(8,128)(2,1)S(1)}, bf16[1,1024,1024]{2,1,0:T(8,128)(2,1)}, u32[]{:S(2)}) copy-start(bf16[1,1024,1024]{2,1,0:T(8,128)(2,1)} %param.14) | copy-start | bytes 6291460
  222.9 1.7 copy-start.5
  250.5 52.3 %copy-start.7 = (bf16[1024,64]{0,1:T(8,128)(2,1)S(1)}, bf16[1024,64]{0,1:T(8,128)(2,1)}, u32[]{:S(2)}) copy-start(bf16[1024,64]{0,1:T(8,128)(2,1)} %param.13) | copy-start | bytes 393220
  289.7 45.2 %copy-start.1 = (bf16[2,512,1536]{2,1,0:T(8,128)(2,1)S(1)}, bf16[2,512,1536]{2,1,0:T(8,128)(2,1)}, u32[]{:S(2)}) copy-start(bf16[2,512,1536]{2,1,0:T(8,128)(2,1)} %param.10) | copy-start | bytes 9437188
  292.0 38.7 %all-to-all-start.2 = ((bf16[64,6,1024]{2,1,0:T(8,128)(2,1)}), bf16[64,6,1024]{2,1,0:T(8,128)(2,1)}, u32[]{:S(2)}, u32[]{:S(2)}) async-start(bf16[64,6,1024]{2,1,0:T(8,128)(2,1)} %reshape.98), calls=%async_computation.3 | async-start | bytes 2097152 | tf_op jit(solution)/shard_map/all_to_all | solution.py:119
Sparse Core Ops, SparseCore 0:
  10.9 133.5 all-gather.1
  250.7 38.9 reduce-scatter.1
